TPU v7x, 512 devices: a whole 4x4x16 slice. The times are simulated.
512 devices in a mesh: brick: 128 (over y, z, core), orb: 4 (over x).
Axes of the slice: x: 4, y: 4, z: 16, core: 2. Of those that a mesh axis runs over, the one named last changes fastest.
Arguments:
- spline_table: float32 [65536, 2048], P('brick', 'orb'), may hold values from -6 to 6
- slot_cell: int32 [128, 256], P('brick'), may hold values from 0 to 124
- slot_offset: int32 [3, 128, 256], P(None, 'brick'), may hold values from 0 to 1023
- inverse: float32 [2048, 65536], P('orb', 'brick'), may hold values from -6 to 6
- old_rows: float32 [16384, 2048], P('brick', 'orb'), may hold values from -12 to 12
- mover_source: int32 [16384], P('brick'), may hold values from 0 to 255, as said below
- mover_column: int32 [16384], P('brick'), may hold values from 0 to 511, as said below
Outputs:
- new_inverse: float32 [2048, 65536], P('orb', 'brick')
- ratios: float32 [10, 16384], P(None, 'brick')
Inputs may be any that keep to these rules, and one draw needn't show every extreme that they name: `mover_source`: at most 2 movers of one device come from one brick, and in every draw some brick serves exactly 2 movers of every device. `mover_column`: the 128 entries of one device are distinct.
All inputs are finite; a program needn't handle non-finite values.
Results may differ from a plain program's by a relative error of at most 0.0003.
Values sent between devices are 32-bit elements; how exact they have to be, the bound alone decides.
No kernel may reach another device: no remote copies, remote signals or barrier semaphores. Data moves between devices by JAX's collectives and lax.ppermute only.
A program may use at most 128 MiB of HBM per device.

v0:
```python
import math

import jax
import jax.numpy as jnp
from jax import lax
from jax.sharding import PartitionSpec as P

ORBITALS = 2048
CB = 5
OFFQ = 1024
GROUP = 4


PRECISE = lax.Precision.HIGHEST
DERIVATIVE_ORDERS = (
    (0, 0, 0),
    (1, 0, 0),
    (0, 1, 0),
    (0, 0, 1),
    (2, 0, 0),
    (0, 2, 0),
    (0, 0, 2),
    (1, 1, 0),
    (1, 0, 1),
    (0, 1, 1),
)


def from_partner(value, axis, distance):
    mask = 2**distance
    pairs = [(source, source ^ mask) for source in range(lax.axis_size(axis))]
    return lax.ppermute(value, axis, pairs)


def spline_basis(param):
    rest = 1.0 - param
    square = param * param
    cubed = square * param
    level_terms = jnp.stack(
        [
            rest * rest * rest / 6.0,
            (3.0 * cubed - 6.0 * square + 4.0) / 6.0,
            (-3.0 * cubed + 3.0 * square + 3.0 * param + 1.0) / 6.0,
            cubed / 6.0,
        ]
    )
    slope_terms = jnp.stack(
        [-0.5 * rest * rest, 1.5 * square - 2.0 * param, -1.5 * square + param + 0.5, 0.5 * square]
    )
    curve_terms = jnp.stack([rest, 3.0 * param - 2.0, 1.0 - 3.0 * param, param])
    return (level_terms, slope_terms, curve_terms)


def axis_weights(cell_pos, param, points):
    offset_grid = jnp.arange(points, dtype=jnp.int32)[None, :] - cell_pos[:, None]
    weight_list = []
    for basis_terms in spline_basis(param):
        weight_row = jnp.zeros(offset_grid.shape, param.dtype)
        for corner in range(4):
            weight_row = weight_row + jnp.where(
                offset_grid == corner, basis_terms[corner][:, None], 0.0
            )
        weight_list.append(weight_row)
    return weight_list


def spline_weights(cell_index, offsets):
    grid_side = CB + 3
    cell_x = cell_index // (CB * CB)
    cell_y = cell_index // CB % CB
    cell_z = cell_index % CB
    params = (offsets.astype(jnp.float32) + 0.5) / OFFQ
    along_x = axis_weights(cell_x, params[0], grid_side)
    along_y = axis_weights(cell_y, params[1], grid_side)
    along_z = axis_weights(cell_z, params[2], grid_side)
    stacked_rows = []
    for order_x, order_y, order_z in DERIVATIVE_ORDERS:
        product_xyz = (
            along_x[order_x][:, :, None, None]
            * along_y[order_y][:, None, :, None]
            * along_z[order_z][:, None, None, :]
        )
        stacked_rows.append(product_xyz.reshape(product_xyz.shape[0], grid_side**3))
    return jnp.stack(stacked_rows)


def local(spline_table, slot_cell, slot_offset, inverse, old_rows, mover_source, mover_column):
    brick_count = lax.axis_size("brick")
    orb_width = spline_table.shape[1]
    mover_count = mover_source.shape[0]
    slot_pairs = slot_cell.shape[1] // brick_count
    delay_rank = GROUP * mover_count
    weights = spline_weights(slot_cell[0], slot_offset[:, 0, :])
    slot_rows = jnp.einsum("rng,gj->rnj", weights, spline_table, precision=PRECISE).reshape(
        10, brick_count, slot_pairs, orb_width
    )
    own_columns = jnp.take(inverse, mover_column, axis=1)
    arrived = lax.all_to_all(slot_rows, "brick", split_axis=1, concat_axis=1, tiled=True)
    picked = jnp.take(
        arrived.reshape(10, brick_count * slot_pairs, orb_width), mover_source, axis=1
    )
    fresh_rows = picked[0]
    ratio_part = jnp.einsum("rmj,jm->rm", picked, own_columns, precision=PRECISE)
    change = fresh_rows - old_rows
    stacked = jnp.stack([change, own_columns.T])
    quarter = lax.axis_index("brick") % GROUP
    for bit_index in range(GROUP.bit_length() - 1):
        partner = from_partner(stacked, "brick", bit_index)
        is_upper = quarter // 2**bit_index % 2 == 1
        stacked = jnp.where(
            is_upper, jnp.concatenate([partner, stacked], 1), jnp.concatenate([stacked, partner], 1)
        )
    change_all = stacked[0]
    column_all = stacked[1]
    product_part = jnp.dot(change_all, inverse, precision=PRECISE)
    product_sum, ratio_sum = lax.psum((product_part, ratio_part), "orb")
    product_z = product_sum / ORBITALS
    mover_index = quarter * mover_count + jnp.arange(mover_count)
    own_core = jnp.take(product_z, mover_column, axis=1) + (
        jnp.arange(delay_rank)[:, None] == mover_index[None, :]
    ).astype(jnp.float32)
    for bit_index in range(GROUP.bit_length() - 1):
        partner = from_partner(own_core, "brick", bit_index)
        is_upper = quarter // 2**bit_index % 2 == 1
        own_core = jnp.where(
            is_upper,
            jnp.concatenate([partner, own_core], 1),
            jnp.concatenate([own_core, partner], 1),
        )
    normal_matrix = jnp.dot(own_core.T, own_core, precision=PRECISE)
    factor = jnp.linalg.cholesky(normal_matrix)
    right_side = jnp.dot(own_core.T, product_z, precision=PRECISE)
    halfway = lax.linalg.triangular_solve(factor, right_side, left_side=True, lower=True)
    solved = lax.linalg.triangular_solve(
        factor, halfway, left_side=True, lower=True, transpose_a=True
    )
    new_inverse = inverse - jnp.einsum("aj,ae->je", column_all, solved, precision=PRECISE)
    return (new_inverse, ratio_sum / math.sqrt(ORBITALS))


def solution(mesh):
    in_specs = (
        P("brick", "orb"),
        P("brick", None),
        P(None, "brick", None),
        P("orb", "brick"),
        P("brick", "orb"),
        P("brick"),
        P("brick"),
    )
    out_specs = (P("orb", "brick"), P(None, "brick"))
    return jax.shard_map(local, mesh=mesh, in_specs=in_specs, out_specs=out_specs, check_vma=False)
```

profile of v0, /device:TPU:8, one launch (start us, length us, event | category | flops | bytes accessed | tf_op | source)
XLA Modules:
  0.0 614.8 jit_solution(11406836245384870055)
XLA Ops:
  9.6 1.9 broadcast_multiply_fusion.2
  13.5 2.1 copy.27
  15.6 2.1 copy.28
  17.7 2.0 copy.29
  19.7 2.0 copy.30
  24.6 1.9 constant_dynamic-update-slice_fusion.8
  26.5 1.9 constant_dynamic-update-slice_fusion.7
  28.4 1.9 constant_dynamic-update-slice_fusion.6
  30.3 1.9 constant_dynamic-update-slice_fusion.5
  32.1 1.9 constant_dynamic-update-slice_fusion.4
  37.3 11.9 %fusion.9 = f32[10,256,512]{2,1,0:T(8,128)} fusion(f32[10,256,512]{2,1,0:T(8,128)} %constant_dynamic-update-slice_fusion, f32[512,512]{1,0:T(8,128)S(1)} %copy-done), kind=kOutput, calls=%fused_computation.31 | convolution fusion | flops 8053063680 | bytes 11534336 | tf_op jit(solution)/shard_map/rng,gj->rnj/dot_general | solution.py:94
  49.2 7.5 %reshape.1336 = f32[10,128,2,512]{3,2,1,0:T(2,128)} reshape(f32[10,256,512]{2,1,0:T(8,128)} %fusion.9) | data formatting | bytes 10485760 | tf_op jit(solution)/shard_map/reshape | solution.py:94
  56.7 6.6 %copy.36 = f32[10,128,2,512]{3,2,0,1:T(2,128)} copy(f32[10,128,2,512]{3,2,1,0:T(2,128)} %reshape.1336) | data formatting | bytes 10485760 | tf_op jit(solution)/shard_map/reshape | solution.py:94
  63.3 20.1 %all-to-all-start = ((f32[10,128,2,512]{3,2,0,1:T(2,128)}), f32[10,128,2,512]{3,2,0,1:T(2,128)}, u32[]{:S(2)}, u32[]{:S(2)}) async-start(f32[10,128,2,512]{3,2,0,1:T(2,128)} %copy.36), calls=%async_computation | async-start | bytes 10485760 | tf_op jit(solution)/shard_map/all_to_all | solution.py:98
  85.3 230.1 %all-to-all-done = f32[10,128,2,512]{3,2,0,1:T(2,128)} async-done(((f32[10,128,2,512]{3,2,0,1:T(2,128)}), f32[10,128,2,512]{3,2,0,1:T(2,128)}, u32[]{:S(2)}, u32[]{:S(2)}) %all-to-all-start) | async-done | bytes 5242912 | tf_op jit(solution)/shard_map/all_to_all | solution.py:98
  315.4 7.4 %copy.37 = f32[10,128,2,512]{3,0,2,1:T(8,128)} copy(f32[10,128,2,512]{3,2,0,1:T(2,128)} %all-to-all-done) | data formatting | bytes 10485760 | tf_op jit(solution)/shard_map/all_to_all | solution.py:98
  322.7 6.2 %gather_fusion = f32[128,10,512]{2,1,0:T(8,128)} fusion(f32[10,256,512]{2,0,1:T(8,128)} %bitcast.104, s32[1024]{0:T(1024)S(1)} %pad_clamp_fusion.1), kind=kCustom, calls=%fused_computation.2 | custom fusion | bytes 5243392 | tf_op jit(solution)/shard_map/jit(_take)/gather | solution.py:99
  328.9 2.6 select_bitcast_fusion
  331.5 1.9 copy-done.2
  333.7 1.9 collective-permute-start
  335.7 1.8 collective-permute-done
  337.7 5.4 collective-permute-start.1
  343.1 23.4 %collective-permute-done.1 = f32[2,256,512]{2,1,0:T(8,128)S(1)} collective-permute-done((f32[2,256,512]{2,1,0:T(8,128)S(1)}, f32[2,256,512]{2,1,0:T(8,128)S(1)}, u32[]{:S(2)}, u32[]{:S(2)}) %collective-permute-start.1) | collective-permute-done | bytes 1048608 | tf_op jit(solution)/shard_map/ppermute | solution.py:32
  366.9 1.3 copy-done.4
  368.2 2.8 fusion
  371.1 55.0 %all-reduce.3.cloned.1.call-done = f32[512,512]{1,0:T(8,128)} async-done(((f32[512,512]{1,0:T(8,128)}), f32[512,512]{1,0:T(8,128)}) %all-reduce.3.cloned.1.call-update) | async-done | bytes 1048592 | tf_op jit(solution)/shard_map/psum | solution.py:116
  426.1 1.3 broadcast_multiply_fusion
  428.6 1.9 collective-permute-start.2
  430.6 1.5 collective-permute-done.2
  432.1 3.5 collective-permute-start.3
  435.6 6.5 %fusion.40 = f32[128,1,10]{2,1,0:T(1,128)S(1)} fusion(f32[10,128,512]{2,0,1:T(8,128)} %copy-done.2, f32[512,128,1]{0,1,2:T(8,128)S(1)} %get-tuple-element.23), kind=kOutput, calls=%fused_computation.71 | convolution fusion | flops 7864320 | bytes 2888704 | tf_op jit(solution)/shard_map/rmj,jm->rm/dot_general | solution.py:103
  442.1 10.1 %psum.15 = f32[10,128]{1,0:T(8,128)S(1)} all-reduce(f32[10,128]{1,0:T(8,128)S(1)} %bitcast.115), channel_id=1, replica_groups=mesh['brick'=128,'orb'=4] {'orb'}, use_global_device_ids=true, to_apply=%region_9.11 | all-reduce | flops 1280 | bytes 10240 | tf_op jit(solution)/shard_map/psum | solution.py:116
  453.6 1.9 fusion.23
  457.0 11.7 %cholesky.104 = f32[128,128]{1,0:T(8,128)S(1)} custom-call(f32[128,128]{1,0:T(8,128)S(1)} %cholesky.266), custom_call_target="Cholesky" | custom-call | tf_op jit(solution)/shard_map/jit(cholesky)/cholesky | solution.py:131
  468.9 9.8 %custom-call.32 = f32[1,128,128]{1,2,0:T(8,128)S(1)} custom-call(f32[1,128,128]{2,1,0:T(8,128)S(1)} %get-tuple-element.34), custom_call_target="InvertDiagBlocksLowerTriangular" | custom-call | tf_op jit(solution)/shard_map/jit(cholesky)/cholesky | solution.py:131
  481.3 12.1 %cholesky.217 = f32[128,128]{1,0:T(8,128)S(1)} custom-call(f32[128,128]{1,0:T(8,128)S(1)} %cholesky.270), custom_call_target="Cholesky" | custom-call | tf_op jit(solution)/shard_map/jit(cholesky)/cholesky | solution.py:131
  493.4 9.8 %custom-call.33 = f32[1,128,128]{1,2,0:T(8,128)S(1)} custom-call(f32[1,128,128]{2,1,0:T(8,128)S(1)} %get-tuple-element.31), custom_call_target="InvertDiagBlocksLowerTriangular" | custom-call | tf_op jit(solution)/shard_map/jit(cholesky)/cholesky | solution.py:131
  504.8 11.7 %cholesky.238 = f32[128,128]{1,0:T(8,128)S(1)} custom-call(f32[128,128]{1,0:T(8,128)S(1)} %cholesky.275), custom_call_target="Cholesky" | custom-call | tf_op jit(solution)/shard_map/jit(cholesky)/cholesky | solution.py:131
  517.2 9.8 %custom-call.34 = f32[1,128,128]{1,2,0:T(8,128)S(1)} custom-call(f32[1,128,128]{2,1,0:T(8,128)S(1)} %get-tuple-element.28), custom_call_target="InvertDiagBlocksLowerTriangular" | custom-call | tf_op jit(solution)/shard_map/jit(cholesky)/cholesky | solution.py:131
  528.4 11.9 %cholesky.255 = f32[128,128]{1,0:T(8,128)S(1)} custom-call(f32[128,128]{1,0:T(8,128)S(1)} %convolution_subtract_fusion.6), custom_call_target="Cholesky" | custom-call | tf_op jit(solution)/shard_map/jit(cholesky)/cholesky | solution.py:131
  544.4 10.3 %while.1 = (s32[]{:T(128)}, f32[512,512]{1,0:T(8,128)S(1)}, s32[4,2]{0,1:T(2,128)S(1)}, f32[4,128,128]{2,1,0:T(8,128)}, s32[]{:T(128)}) while((s32[]{:T(128)}, f32[512,512]{1,0:T(8,128)S(1)}, s32[4,2]{0,1:T(2,128)S(1)}, f32[4,128,128]{2,1,0:T(8,128)}, s32[]{:T(128)}) %tuple.92), condition=%wide.while_cond, body=%wide.while_body.sunk | while | flops 2 | bytes 132705 | solution.py:134
  545.0 2.0 bitcast_dynamic-update-slice_fusion.2
  547.6 2.0 bitcast_dynamic-update-slice_fusion.2
  550.1 2.0 bitcast_dynamic-update-slice_fusion.2
  552.7 2.0 bitcast_dynamic-update-slice_fusion.2
  554.7 40.1 %custom-call.35 = f32[4,128,128]{1,2,0:T(8,128)S(1)} custom-call(f32[4,128,128]{2,1,0:T(8,128)} %get-tuple-element.10), custom_call_target="InvertDiagBlocksLowerTriangular" | custom-call | tf_op jit(solution)/shard_map/triangular_solve | solution.py:134
  594.8 3.7 fusion.22
  604.9 2.9 convolution_subtract_fusion
  (116 shorter events, 33.7 us)
Async XLA Ops:
  7.2 30.2 %copy-start = (f32[512,512]{1,0:T(8,128)S(1)}, f32[512,512]{1,0:T(8,128)}, u32[]{:S(2)}) copy-start(f32[512,512]{1,0:T(8,128)} %param.9) | copy-start | bytes 3145732
  13.5 9.4 %copy-start.8 = (f32[256,8,8,8]{0,3,2,1:T(8,128)S(1)}, f32[256,8,8,8]{0,3,2,1:T(8,128)}, u32[]{:S(2)}) copy-start(f32[256,8,8,8]{0,3,2,1:T(8,128)} %get-tuple-element.46) | copy-start | bytes 1572868
  63.3 20.7 %copy-start.3 = (f32[512,512]{1,0:T(8,128)S(1)}, f32[512,512]{1,0:T(8,128)}, u32[]{:S(2)}) copy-start(f32[512,512]{1,0:T(8,128)} %param.12) | copy-start | bytes 3145732
  63.3 21.0 %copy-start.12 = (s32[128]{0:T(128)S(1)}, s32[128]{0:T(128)}, u32[]{:S(2)}) copy-start(s32[128]{0:T(128)} %param.15) | copy-start | bytes 1540
  63.3 21.8 %copy-start.11 = (s32[128]{0:T(128)S(1)}, s32[128]{0:T(128)}, u32[]{:S(2)}) copy-start(s32[128]{0:T(128)} %param.14) | copy-start | bytes 1540
  63.3 252.1 %all-to-all-start = ((f32[10,128,2,512]{3,2,0,1:T(2,128)}), f32[10,128,2,512]{3,2,0,1:T(2,128)}, u32[]{:S(2)}, u32[]{:S(2)}) async-start(f32[10,128,2,512]{3,2,0,1:T(2,128)} %copy.36), calls=%async_computation | async-start | bytes 10485760 | tf_op jit(solution)/shard_map/all_to_all | solution.py:98
  83.5 342.6 %all-reduce.3.cloned.1.call-start = ((), (), s32[]{:S(2)}) async-start(), calls=%async_computation.1 | async-start | bytes 2097152 | tf_op jit(solution)/shard_map/psum | solution.py:116
  328.9 4.7 copy-start.10
  331.5 1.9 copy-start.2
  333.7 3.8 collective-permute-start
  337.7 28.9 %collective-permute-start.1 = (f32[2,256,512]{2,1,0:T(8,128)S(1)}, f32[2,256,512]{2,1,0:T(8,128)S(1)}, u32[]{:S(2)}, u32[]{:S(2)}) collective-permute-start(f32[2,256,512]{2,1,0:T(8,128)S(1)} %maximum_select_fusion.1), channel_id=1, source_target_pairs={{0,8},{4,12},{8,0},{12,4},{16,24},{20,28},{24,16},{28,20},{32,40},... | collective-permute-start | bytes 3145736 | tf_op jit(solution)/shard_map/ppermute | solution.py:32
  366.9 1.3 copy-start.4
  428.6 3.4 collective-permute-start.2
  432.1 20.7 %copy-start.7 = (f32[512,256]{0,1:T(8,128)}, f32[512,256]{0,1:T(8,128)S(1)}, u32[]{:S(2)}) copy-start(f32[512,256]{0,1:T(8,128)S(1)} %maximum_select_fusion.5) | copy-start | bytes 1572868
  432.1 20.7 %collective-permute-start.3 = (f32[512,256]{0,1:T(8,128)S(1)}, f32[512,256]{0,1:T(8,128)S(1)}, u32[]{:S(2)}, u32[]{:S(2)}) collective-permute-start(f32[512,256]{0,1:T(8,128)S(1)} %maximum_select_fusion.5), channel_id=1, source_target_pairs={{0,8},{4,12},{8,0},{12,4},{16,24},{20,28},{24,16},{28,20},{32,40},... | collective-permute-start | bytes 1572872 | tf_op jit(solution)/shard_map/ppermute | solution.py:32
  452.8 0.8 copy-start.9
  456.1 1.0 copy-start.6
  599.4 5.5 copy-start.5
  601.4 6.4 %copy-start.1 = (f32[512,512]{1,0:T(8,128)S(1)}, f32[512,512]{1,0:T(8,128)}, u32[]{:S(2)}) copy-start(f32[512,512]{1,0:T(8,128)} %param.9) | copy-start | bytes 3145732
Sparse Core Ops, SparseCore 0:
  371.2 54.8 all-reduce.2
where the time goes:
time: 624 us; the launch traced here: 615 us
  waiting for transfers between devices  312 us (50%)
  other arithmetic  129 us (21%)
  local copies, waits for them, and re-layouts  71.7 us (11%)
  matrix products  41.3 us (7%)
  starting transfers between devices  33.4 us (5%)
  between operations  17.5 us (3%)
  blocking collectives  10.1 us (2%)
    all_to_all x1, waiting for transfers between devices, local(): lax.all_to_all(slot_rows, 'brick', split_axis=1, concat_axis=1, tiled=True)  230 us
    another operation x14, other arithmetic, local(): factor = jnp.linalg.cholesky(normal_matrix)  79 us
    psum x1, waiting for transfers between devices, local(): product_sum, ratio_sum = lax.psum((product_part, ratio_part), 'orb')  55 us
    another operation x3, other arithmetic, local(): lax.linalg.triangular_solve(factor, halfway, left_side=True, lower=True,...  40.3 us
    ppermute x4, waiting for transfers between devices, from_partner(): return lax.ppermute(value, axis, pairs)  26.7 us
    all_to_all x1, starting transfers between devices, local(): lax.all_to_all(slot_rows, 'brick', split_axis=1, concat_axis=1, tiled=True)  20.1 us
    unnamed x36, local copies, waits for them, and re-layouts  18.1 us
    reshape x2, local copies, waits for them, and re-layouts, local(): jnp.einsum('rng,gj->rnj', weights, spline_table, precision=PRECISE)  14.1 us
  transfers between devices with their start and end apart: 6, of which 5 were waited for; matrix products, arithmetic and copies ran while one was open for 1% of the time, Pallas kernels for 0%

commit v1 on v0

v1 whole, which is shorter than its diff:
```python
import math

import jax
import jax.numpy as jnp
from jax import lax
from jax.experimental import pallas as pl
from jax.experimental.pallas import tpu as pltpu
from jax.sharding import Mesh
from jax.sharding import PartitionSpec as P

ORBITALS = 2048
CB = 5
OFFQ = 1024
GROUP = 4
MOVERS = 128
SLOTS = 256
WIDTH = 512
GRID_SIDE = CB + 3
DELAY = 512
ORB = 4
CHUNK = MOVERS // ORB
LANES = 128
PARTS = WIDTH // LANES

F32 = jnp.float32
BF16 = jnp.bfloat16
DERIVATIVE_ORDERS = (
    (0, 0, 0),
    (1, 0, 0),
    (0, 1, 0),
    (0, 0, 1),
    (2, 0, 0),
    (0, 2, 0),
    (0, 0, 2),
    (1, 1, 0),
    (1, 0, 1),
    (0, 1, 1),
)
NN = (((1,), (0,)), ((), ()))
NT = (((1,), (1,)), ((), ()))
TN = (((0,), (0,)), ((), ()))

PARAMS = pltpu.CompilerParams(vmem_limit_bytes=48 * 1024 * 1024)


def call(body, out_shapes, scratch=(), scalars=0, loose=0, passes=4):
    def run(*operands):
        held = len(operands) - scalars - loose
        spaces = [pltpu.SMEM] * scalars + [pltpu.VMEM] * held + [pl.ANY] * loose
        return pl.pallas_call(
            body,
            in_specs=[pl.BlockSpec(memory_space=space) for space in spaces],
            out_specs=[pl.BlockSpec(memory_space=pltpu.VMEM) for _ in out_shapes],
            out_shape=[jax.ShapeDtypeStruct(shape, F32) for shape in out_shapes],
            scratch_shapes=list(scratch),
            compiler_params=PARAMS,
            cost_estimate=pl.CostEstimate(
                flops=passes * 2 * DELAY**3, transcendentals=0, bytes_accessed=4 * DELAY**2
            ),
        )(*operands)

    return run


def halves(value):
    high = value.astype(BF16)
    return high, (value - high.astype(F32)).astype(BF16)


def mm(left, right, dims):
    return lax.dot_general(left, right, dims, preferred_element_type=F32)


def mm3(left, right, dims):
    left_high, left_low = halves(left)
    right_high, right_low = halves(right)
    return (
        mm(left_high, right_low, dims) + mm(left_low, right_high, dims)
    ) + mm(left_high, right_high, dims)


def select_rows(choice, right, dims):
    high, low = halves(right)
    return mm(choice, high, dims) + mm(choice, low, dims)


def axis_weights(cell, param):
    rest = 1.0 - param
    square = param * param
    cubed = square * param
    level = (
        rest * rest * rest / 6.0,
        (3.0 * cubed - 6.0 * square + 4.0) / 6.0,
        (-3.0 * cubed + 3.0 * square + 3.0 * param + 1.0) / 6.0,
        cubed / 6.0,
    )
    slope = (
        -0.5 * rest * rest,
        1.5 * square - 2.0 * param,
        -1.5 * square + param + 0.5,
        0.5 * square,
    )
    curve = (rest, 3.0 * param - 2.0, 1.0 - 3.0 * param, param)
    corner_of = lax.broadcasted_iota(jnp.int32, cell.shape, 0).astype(F32) - cell
    out = []
    for terms in (level, slope, curve):
        row = jnp.zeros(cell.shape, F32)
        for corner in range(4):
            row = row + jnp.where(corner_of == float(corner), terms[corner], 0.0)
        out.append(row)
    return out


def slot_values(cell_ref, offset_ref):
    shape = (GRID_SIDE, SLOTS)
    cell = jnp.broadcast_to(cell_ref[...].astype(F32), shape)
    cell_x = jnp.floor((cell + 0.5) * (1.0 / (CB * CB)))
    rest = cell - cell_x * (CB * CB)
    cell_y = jnp.floor((rest + 0.5) * (1.0 / CB))
    cell_z = rest - cell_y * CB
    params = [
        (jnp.broadcast_to(offset_ref[axis].astype(F32), shape) + 0.5) * (1.0 / OFFQ)
        for axis in range(3)
    ]
    return [cell_x, cell_y, cell_z], params


def slot_rows(cell_ref, offset_ref, table_ref):
    cells, params = slot_values(cell_ref, offset_ref)
    along_x, along_y, along_z = [axis_weights(c, t)[0] for c, t in zip(cells, params)]
    pieces = []
    for gx in range(GRID_SIDE):
        for gy in range(GRID_SIDE):
            pieces.append((along_x[gx : gx + 1] * along_y[gy : gy + 1]) * along_z)
    return mm3(jnp.concatenate(pieces, axis=0), table_ref[...], TN)


def as_column(row):
    shape = (MOVERS, MOVERS)
    diagonal = lax.broadcasted_iota(jnp.int32, shape, 0) == lax.broadcasted_iota(
        jnp.int32, shape, 1
    )
    return jnp.sum(jnp.where(diagonal, jnp.broadcast_to(row, shape), 0.0), axis=1, keepdims=True)


def lane_of(source):
    shape = (MOVERS, MOVERS)
    earlier = lax.broadcasted_iota(jnp.int32, shape, 0) < lax.broadcasted_iota(jnp.int32, shape, 1)
    same = jnp.broadcast_to(as_column(source), shape) == jnp.broadcast_to(source, shape)
    taken = jnp.sum(jnp.where(earlier & same, 1.0, 0.0), axis=0, keepdims=True)
    pair = source - 2.0 * jnp.floor((source + 0.5) * 0.5)
    swapped = taken > 0.5
    return jnp.where(swapped, source + 1.0 - 2.0 * pair, source), jnp.where(swapped, 1.0, 0.0)


def hot(match):
    return jnp.where(match, 1.0, 0.0).astype(BF16)


def send_body(
    cell_ref, offset_ref, source_ref, column_ref, table_ref, inverse_ref, own_ref, out_ref
):
    source = source_ref[...].astype(F32)
    column = as_column(column_ref[...].astype(F32))
    position = lax.broadcasted_iota(jnp.int32, (MOVERS, WIDTH), 1).astype(F32)
    own = select_rows(hot(position == column), inverse_ref[...], NT)
    own_ref[...] = own
    lane, _ = lane_of(source)
    slot = lax.broadcasted_iota(jnp.int32, (SLOTS, MOVERS), 0).astype(F32)
    sent = select_rows(hot(slot == lane), own, NN)
    rows = slot_rows(cell_ref, offset_ref, table_ref)
    for part in range(PARTS):
        span = slice(part * LANES, (part + 1) * LANES)
        out_ref[pl.ds(part, SLOTS, stride=2 * PARTS), :] = rows[:, span]
        out_ref[pl.ds(PARTS + part, SLOTS, stride=2 * PARTS), :] = sent[:, span]


def gather_body(place_ref, own_ref, far_ref, pair_ref, out_ref):
    group = place_ref[0]
    out_ref[group] = own_ref[...]
    out_ref[group ^ 2] = far_ref[...]
    out_ref[group ^ 1] = pair_ref[0]
    out_ref[group ^ 3] = pair_ref[1]


def change_body(source_ref, arrived_ref, old_ref, columns_ref, *refs):
    out_ref = refs[-1]
    source = as_column(source_ref[...].astype(F32))
    position = lax.broadcasted_iota(jnp.int32, (MOVERS, SLOTS), 1).astype(F32)
    choice = hot(position == source)
    rows = jnp.concatenate(
        [
            select_rows(choice, arrived_ref[pl.ds(part, SLOTS, stride=2 * PARTS), :], NN)
            for part in range(PARTS)
        ],
        axis=1,
    )
    change = rows - old_ref[...]
    core = mm3(change, columns_ref[...], NT) * (1.0 / ORBITALS)
    for member in range(ORB):
        span = slice(member * CHUNK, (member + 1) * CHUNK)
        out_ref[member, 0:CHUNK] = change[span]
        out_ref[member, CHUNK : 2 * CHUNK] = core[span]


def middle_body(parts_ref, core_ref, change_ref):
    core = [parts_ref[member, CHUNK : 2 * CHUNK] for member in range(ORB)]
    total = (core[0] + core[1]) + (core[2] + core[3])
    for member in range(GROUP * ORB):
        core_ref[member] = total
    for member in range(ORB):
        change_ref[member] = parts_ref[member, 0:CHUNK]


def product_body(place_ref, own_ref, far_ref, pair_ref, here_ref, *refs):
    other_refs, out_ref, rows_ref = refs[:-2], refs[-2], refs[-1]
    group = place_ref[0]
    orb = place_ref[1]
    for member in range(ORB):
        for block, part in (
            (group, own_ref[member]),
            (group ^ 2, far_ref[member]),
            (group ^ 1, pair_ref[0, member]),
            (group ^ 3, pair_ref[1, member]),
        ):
            rows_ref[member, pl.ds(pl.multiple_of(block * CHUNK, CHUNK), CHUNK), :] = part
    total = mm3(rows_ref[orb], here_ref[...], NN)
    for step, other_ref in enumerate(other_refs):
        total += mm3(rows_ref[orb ^ (step + 1)], other_ref[...], NN)
    out_ref[...] = total * (1.0 / ORBITALS)


def total_of(parts_ref):
    return (parts_ref[0] + parts_ref[1]) + (parts_ref[2] + parts_ref[3])


BF16_STEPS = 24
SPLIT_STEPS = 8
FULL_STEPS = 64
COARSE = 0.01
FINE = 1e-5


def solve_body(core_ref, columns_ref, *refs):
    out_ref, full_ref, guess_ref, rest_ref = refs[-4:]
    shape = (DELAY, DELAY)
    identity = jnp.where(
        lax.broadcasted_iota(jnp.int32, shape, 0) == lax.broadcasted_iota(jnp.int32, shape, 1),
        1.0,
        0.0,
    )
    full_ref[...] = core_ref[...] + identity
    size = jnp.abs(full_ref[...])
    bound = jnp.max(jnp.sum(size, axis=0)) * jnp.max(jnp.sum(size, axis=1))

    def start():
        guess_ref[...] = full_ref[...].T * (1.0 / bound)

    def remain(product):
        left = (
            jnp.where(
                lax.broadcasted_iota(jnp.int32, shape, 0)
                == lax.broadcasted_iota(jnp.int32, shape, 1),
                1.0,
                0.0,
            )
            - product
        )
        rest_ref[...] = left
        return jnp.sum(left * left)

    def coarse_step(carry):
        step, _, last = carry
        guess = guess_ref[...].astype(BF16)
        size = remain(mm(full_ref[...].astype(BF16), guess, NN))
        guess_ref[...] += mm(guess, rest_ref[...].astype(BF16), NN)
        return step + 1, last, size

    def coarse_more(carry):
        step, before, last = carry
        stalled = (last < 0.5) & (last > 0.5 * before)
        return (step < BF16_STEPS) & (last > COARSE) & (last < 1e4) & jnp.logical_not(stalled)

    def split_step(carry):
        step, _ = carry
        size = remain(mm3(full_ref[...], guess_ref[...], NN))
        guess_ref[...] += mm(guess_ref[...].astype(BF16), rest_ref[...].astype(BF16), NN)
        return step + 1, size

    def full_step(carry):
        step, _ = carry
        size = remain(
            lax.dot_general(
                full_ref[...],
                guess_ref[...],
                NN,
                precision=lax.Precision.HIGHEST,
                preferred_element_type=F32,
            )
        )
        guess_ref[...] += lax.dot_general(
            guess_ref[...],
            rest_ref[...],
            NN,
            precision=lax.Precision.HIGHEST,
            preferred_element_type=F32,
        )
        return step + 1, size

    start()
    _, _, coarse = lax.while_loop(coarse_more, coarse_step, (0, F32(1e3), F32(1e3)))
    usable = coarse < 0.5
    _, split = lax.while_loop(
        lambda c: (c[0] < SPLIT_STEPS) & (c[1] > FINE) & (c[1] < 1e4),
        split_step,
        (jnp.where(usable, 0, SPLIT_STEPS), F32(1e3)),
    )
    settled = split <= FINE

    @pl.when(jnp.logical_not(settled))
    def _():
        start()

    lax.while_loop(
        lambda c: (c[0] < FULL_STEPS) & (c[1] > 1e-9),
        full_step,
        (jnp.where(settled, FULL_STEPS, 0), F32(1e3)),
    )
    out_ref[...] = mm3(columns_ref[...], guess_ref[...], TN)


def finish_body(place_ref, inverse_ref, left_ref, own_ref, *refs):
    other_refs, out_ref, product_ref = refs[:-2], refs[-2], refs[-1]
    orb = place_ref[1]
    for step, part_ref in enumerate((own_ref, *other_refs)):
        first = (orb ^ step) * CHUNK
        for group in range(GROUP):
            row = pl.multiple_of(group * MOVERS + first, CHUNK)
            product_ref[pl.ds(row, CHUNK), :] = part_ref[group * CHUNK : (group + 1) * CHUNK]
    out_ref[...] = inverse_ref[...] - mm3(left_ref[...], product_ref[...], NN)


def ratio_values(grid_ref, cells, params):
    along = [axis_weights(c, t) for c, t in zip(cells, params)]
    side = GRID_SIDE
    by_x = {}
    for order in range(3):
        planes = []
        for gy in range(side):
            total = None
            for gx in range(side):
                first = (gx * side + gy) * side
                term = along[0][order][gx : gx + 1] * grid_ref[first : first + side, :]
                total = term if total is None else total + term
            planes.append(total)
        by_x[order] = planes
    by_xy = {}
    for order_x, order_y in ((0, 0), (1, 0), (0, 1), (2, 0), (0, 2), (1, 1)):
        total = None
        for gy in range(side):
            term = along[1][order_y][gy : gy + 1] * by_x[order_x][gy]
            total = term if total is None else total + term
        by_xy[order_x, order_y] = total
    return [
        jnp.sum(along[2][oz] * by_xy[ox, oy], axis=0, keepdims=True)
        for ox, oy, oz in DERIVATIVE_ORDERS
    ]


def ratio_body(cell_ref, offset_ref, table_ref, arrived_ref, *refs):
    out_ref, grid_ref, turn_ref = refs[-3:]
    columns = jnp.concatenate(
        [
            arrived_ref[pl.ds(PARTS + part, SLOTS, stride=2 * PARTS), :]
            for part in range(PARTS)
        ],
        axis=1,
    )
    grid_ref[...] = mm3(table_ref[...], columns, NT)
    cells, params = slot_values(cell_ref, offset_ref)
    odd = lax.broadcasted_iota(jnp.int32, (GRID_SIDE, SLOTS), 1) % 2 == 1

    def other(value):
        return jnp.where(odd, pltpu.roll(value, 1, 1), pltpu.roll(value, SLOTS - 1, 1))

    values = ratio_values(grid_ref, cells, params)
    values += ratio_values(grid_ref, [other(c) for c in cells], [other(t) for t in params])
    values.append(jnp.zeros((LANES - len(values), SLOTS), F32))
    turn_ref[...] = jnp.concatenate(values, axis=0).T
    half = SLOTS // 2
    out_ref[...] = turn_ref[pl.ds(0, half, stride=2), :] + pltpu.roll(
        turn_ref[pl.ds(1, half, stride=2), :], LANES // 2, 1
    )


COUNT = len(DERIVATIVE_ORDERS)


def ratio_pick_body(source_ref, values_ref, out_ref):
    lane, swapped = lane_of(source_ref[...].astype(F32))
    brick = jnp.floor((lane + 0.5) * 0.5)
    pair = lane - 2.0 * brick
    position = lax.broadcasted_iota(jnp.int32, (MOVERS, MOVERS), 0).astype(F32)
    choice = hot(position == brick)
    value = values_ref[...]
    high = value.astype(BF16)
    rest = value - high.astype(F32)
    middle = rest.astype(BF16)
    low = (rest - middle.astype(F32)).astype(BF16)
    picked = (mm(low, choice, TN) + mm(middle, choice, TN)) + mm(high, choice, TN)
    half = LANES // 2

    both = []
    for first in (0, half):
        both.append((picked[first : first + COUNT], picked[first + COUNT : first + 2 * COUNT]))
    chosen = []
    for straight, crossed in both:
        chosen.append(jnp.where(swapped > 0.5, crossed, straight))
    value = jnp.where(pair > 0.5, chosen[1], chosen[0])
    out = jnp.concatenate([value, jnp.zeros((16 - COUNT, MOVERS), F32)], axis=0)
    for member in range(ORB):
        out_ref[member] = out


def ratio_sum_body(parts_ref, out_ref):
    out_ref[...] = total_of(parts_ref)[:COUNT] * (1.0 / math.sqrt(ORBITALS))


def exchange(value, axes):
    return lax.all_to_all(value, axes, 0, 0, tiled=True)


def swap(value, axis, mask):
    return lax.ppermute(value, axis, [(device, device ^ mask) for device in range(4)])


def local(spline_table, slot_cell, slot_offset, inverse, old_rows, mover_source, mover_column):
    source = mover_source.reshape(1, MOVERS)
    column = mover_column.reshape(1, MOVERS)
    brick = ("walker", "group")
    tiles = SLOTS * 2 * PARTS
    place = jnp.stack([lax.axis_index("group"), lax.axis_index("orb")]).astype(jnp.int32)

    own_columns, sent = call(send_body, [(MOVERS, WIDTH), (tiles, LANES)])(
        slot_cell, slot_offset, source, column, spline_table, inverse
    )
    arrived = exchange(sent.reshape(tiles // 16, 16, LANES), brick).reshape(tiles, LANES)

    far_columns = swap(own_columns, "group", 2)
    pair_columns = swap(jnp.stack([own_columns, far_columns]), "group", 1)
    (columns,) = call(gather_body, [(GROUP, MOVERS, WIDTH)], scalars=1)(
        place, own_columns, far_columns, pair_columns
    )
    columns = columns.reshape(DELAY, WIDTH)
    kept, _ = lax.optimization_barrier((inverse, own_columns))
    inverses = [swap(kept, "orb", mask) for mask in range(1, ORB)]

    (parts,) = call(change_body, [(ORB, 2 * CHUNK, WIDTH)], loose=ORB - 1)(
        source, arrived, old_rows, columns, *inverses
    )
    core_rows, change = call(middle_body, [(GROUP * ORB, CHUNK, DELAY), (ORB, CHUNK, WIDTH)])(
        exchange(parts, "orb")
    )
    core = exchange(core_rows, ("group", "orb")).reshape(DELAY, DELAY)

    far_change = swap(change, "group", 2)
    pair_change = swap(jnp.stack([change, far_change]), "group", 1)
    (product,) = call(
        product_body, [(MOVERS, WIDTH)], [pltpu.VMEM((ORB, MOVERS, WIDTH), F32)], scalars=1
    )(place, change, far_change, pair_change, inverse, *inverses)
    products = [swap(product, "orb", mask) for mask in range(1, ORB)]

    (ratio_part,) = call(
        ratio_body,
        [(SLOTS // 2, LANES)],
        [pltpu.VMEM((GRID_SIDE**3, SLOTS), F32), pltpu.VMEM((SLOTS, LANES), F32)],
        loose=1,
    )(slot_cell, slot_offset, spline_table, arrived, core)
    ratio_back = exchange(ratio_part.reshape(SLOTS // 2, 1, LANES), brick)

    square = pltpu.VMEM((DELAY, DELAY), F32)
    (left,) = call(solve_body, [(WIDTH, DELAY)], [square, square, square], loose=2, passes=64)(
        core, columns, ratio_part, product
    )
    (new_inverse,) = call(
        finish_body, [(WIDTH, WIDTH)], [pltpu.VMEM((DELAY, WIDTH), F32)], scalars=1
    )(place, inverse, left, product, *products)

    (ratio_own,) = call(ratio_pick_body, [(ORB, 16, MOVERS)])(
        source, ratio_back.reshape(SLOTS // 2, LANES)
    )
    (ratios,) = call(ratio_sum_body, [(COUNT, MOVERS)])(exchange(ratio_own, "orb"))
    return new_inverse, ratios


def solution(mesh):
    devices = mesh.devices
    inner = Mesh(
        devices.reshape(devices.shape[0] // GROUP, GROUP, devices.shape[1]),
        ("walker", "group", "orb"),
    )
    brick = ("walker", "group")
    in_specs = (
        P(brick, "orb"),
        P(brick, None),
        P(None, brick, None),
        P("orb", brick),
        P(brick, "orb"),
        P(brick),
        P(brick),
    )
    out_specs = (P("orb", brick), P(None, brick))
    return jax.shard_map(local, mesh=inner, in_specs=in_specs, out_specs=out_specs, check_vma=False)
```

time: 624 us -> 194 us (0.31); the launches traced: 615 us -> 192 us
  waiting for transfers between devices: 312 us -> 61.6 us
  other arithmetic: 129 us -> 0.98 us
  local copies, waits for them, and re-layouts: 71.7 us -> 12.9 us
  matrix products: 41.3 us -> 0 us
  starting transfers between devices: 33.4 us -> 74.3 us
  Pallas kernels: 0 us -> 28 us
  between operations: 17.5 us -> 0.91 us
    all_to_all x1 -> x4, waiting for transfers between devices: 230 us -> 2.29 us  [exchange(): return lax.all_to_all(value, axes, 0, 0, tiled=True)]
    another operation x19 -> x3, other arithmetic: 119 us -> 0.98 us  [the longest x1 0.87 us: local(): pair_columns = swap(jnp.stack([own_columns, far_columns]), 'group', 1)]
    psum x1 -> x0, waiting for transfers between devices: 55 us -> none  [local(): product_sum, ratio_sum = lax.psum((product_part, ratio_part), 'orb')]
    ppermute x4 -> x10, waiting for transfers between devices: 26.7 us -> 59.3 us  [swap(): lax.ppermute(value, axis, [(device, device ^ mask) for device in range(4)])]
    dot_general x6 -> x0, matrix products: 29.7 us -> none  [the longest x1 11.9 us: local(): jnp.einsum('rng,gj->rnj', weights, spline_table, precision=PRECISE)]
    pallas_call x0 -> x10, Pallas kernels: none -> 28 us  [run(): pl.pallas_call(body, in_specs=[pl.BlockSpec(memory_space=space) for space...]
    all_to_all x1 -> x4, starting transfers between devices: 20.1 us -> 43.7 us  [exchange(): return lax.all_to_all(value, axes, 0, 0, tiled=True)]
    ppermute x4 -> x10, starting transfers between devices: 12.7 us -> 30.5 us  [swap(): lax.ppermute(value, axis, [(device, device ^ mask) for device in range(4)])]
  transfers between devices with their start and end apart: 6 -> 14, of which waited for: 5 -> 5; matrix products, arithmetic and copies ran while one was open for 1% -> 1% of each run, Pallas kernels for 0% -> 13%
where the time goes in v1:
time: 194 us; the launch traced here: 192 us
  starting transfers between devices  74.3 us (38%)
  waiting for transfers between devices  61.6 us (32%)
  Pallas kernels  28 us (14%)
  blocking collectives  13.9 us (7%)
  local copies, waits for them, and re-layouts  12.9 us (7%)
    ppermute x10, waiting for transfers between devices, swap(): lax.ppermute(value, axis, [(device, device ^ mask) for device in range(4)])  59.3 us
    all_to_all x4, starting transfers between devices, exchange(): return lax.all_to_all(value, axes, 0, 0, tiled=True)  43.7 us
    ppermute x10, starting transfers between devices, swap(): lax.ppermute(value, axis, [(device, device ^ mask) for device in range(4)])  30.5 us
    pallas_call x10, Pallas kernels, run(): pl.pallas_call(body, in_specs=[pl.BlockSpec(memory_space=space) for space...  28 us
    all_to_all x1, blocking collectives, exchange(): return lax.all_to_all(value, axes, 0, 0, tiled=True)  13.9 us
    unnamed x38, local copies, waits for them, and re-layouts  12.9 us
  transfers between devices with their start and end apart: 14, of which 5 were waited for; matrix products, arithmetic and copies ran while one was open for 1% of the time, Pallas kernels for 13%

profile of v1, /device:TPU:8, one launch (start us, length us, event | category | flops | bytes accessed | tf_op | source)
XLA Modules:
  0.0 192.5 jit_solution(15071836994087035847)
XLA Ops:
  0.7 0.7 copy-done.16
  1.3 1.2 copy-done
  2.5 1.2 copy-done.14
  3.8 0.7 copy-done.17
  4.5 0.7 copy-done.18
  5.1 2.2 %shard_map.86 = (f32[128,512]{1,0:T(8,128)S(1)}, f32[2048,128]{1,0:T(8,128)}) custom-call(s32[1,256]{1,0:T(1,128)S(1)} %copy-done.17, s32[3,1,256]{2,1,0:T(1,128)S(1)} %copy-done.16, s32[1,128]{1,0:T(1,128)S(1)} %bitcast.25, s32[1,128]{1,0:T(1,128)S(1)} %bitcast.28, f32[512,512]{1,0:T(8,128)S(1)} %copy-done.14, f32[512,512]{1,0:T(8,128)S(1)} %copy-done), custom_call_target="tpu_custom_call" | custom-call | flops 1073741824 | bytes 1048576 | tf_op jit(solution)/shard_map/pallas_call | solution.py:50
  7.3 19.7 %all-to-all-start = ((f32[128,16,128]{2,1,0:T(8,128)}), f32[128,16,128]{2,1,0:T(8,128)S(1)}, u32[]{:S(2)}, u32[]{:S(2)}) async-start(f32[128,16,128]{2,1,0:T(8,128)} %bitcast.4), calls=%async_computation | async-start | bytes 2097152 | tf_op jit(solution)/shard_map/all_to_all | solution.py:430
  27.1 4.7 %collective-permute-start.4 = (f32[512,512]{1,0:T(8,128)S(1)}, f32[512,512]{1,0:T(8,128)S(1)}, u32[]{:S(2)}, u32[]{:S(2)}) collective-permute-start(f32[512,512]{1,0:T(8,128)S(1)} %copy-done.1), channel_id=1, source_target_pairs={{0,3},{1,2},{2,1},{3,0},{4,7},{5,6},{6,5},{7,4},{8,11},{9,10},{10,... | collective-permute-start | bytes 3145736 | tf_op jit(solution)/shard_map/ppermute | solution.py:434
  31.7 2.7 %collective-permute-start.3 = (f32[512,512]{1,0:T(8,128)S(1)}, f32[512,512]{1,0:T(8,128)}, u32[]{:S(2)}, u32[]{:S(2)}) collective-permute-start(f32[512,512]{1,0:T(8,128)S(1)} %copy-done.1), channel_id=1, source_target_pairs={{0,2},{1,3},{2,0},{3,1},{4,6},{5,7},{6,4},{7,5},{8,10},{9,11},{10,... | collective-permute-start | bytes 3145736 | tf_op jit(solution)/shard_map/ppermute | solution.py:434
  34.5 2.4 %collective-permute-start.2 = (f32[512,512]{1,0:T(8,128)S(1)}, f32[512,512]{1,0:T(8,128)}, u32[]{:S(2)}, u32[]{:S(2)}) collective-permute-start(f32[512,512]{1,0:T(8,128)S(1)} %copy-done.1), channel_id=1, source_target_pairs={{0,1},{1,0},{2,3},{3,2},{4,5},{5,4},{6,7},{7,6},{8,9},{9,8},{10,11... | collective-permute-start | bytes 3145736 | tf_op jit(solution)/shard_map/ppermute | solution.py:434
  36.9 3.4 %collective-permute-start = (f32[128,512]{1,0:T(8,128)S(1)}, f32[128,512]{1,0:T(8,128)S(1)}, u32[]{:S(2)}, u32[]{:S(2)}) collective-permute-start(f32[128,512]{1,0:T(8,128)S(1)} %get-tuple-element.8.own_ref), channel_id=1, source_target_pairs={{0,8},{4,12},{8,0},{12,4},{1,9},{5,13},{9,1},{13,5},{2,10},{6,14},... | collective-permute-start | bytes 786440 | tf_op jit(solution)/shard_map/ppermute | solution.py:434
  40.3 39.1 %collective-permute-done.far_ref = f32[128,512]{1,0:T(8,128)S(1)} collective-permute-done((f32[128,512]{1,0:T(8,128)S(1)}, f32[128,512]{1,0:T(8,128)S(1)}, u32[]{:S(2)}, u32[]{:S(2)}) %collective-permute-start) | collective-permute-done | bytes 262176 | tf_op jit(solution)/shard_map/ppermute | solution.py:434
  79.4 0.9 pad_maximum_fusion
  80.3 1.9 collective-permute-start.1
  82.2 0.1 pad_add_fusion.place_ref
  82.3 2.1 %collective-permute-done.1.pair_ref = f32[2,128,512]{2,1,0:T(8,128)} collective-permute-done((f32[2,128,512]{2,1,0:T(8,128)}, f32[2,128,512]{2,1,0:T(8,128)}, u32[]{:S(2)}, u32[]{:S(2)}) %collective-permute-start.1) | collective-permute-done | bytes 524320 | tf_op jit(solution)/shard_map/ppermute | solution.py:434
  84.4 0.9 copy-done.10
  85.4 0.9 copy-done.12
  86.3 1.1 shard_map.87
  87.5 1.0 copy-done.5
  88.4 0.0 collective-permute-done.4.refs_2_
  88.5 1.2 copy-done.6
  89.7 0.9 shard_map.88
  90.6 13.9 %all_to_all.25.parts_ref = f32[4,64,512]{2,1,0:T(8,128)S(1)} all-to-all(f32[4,64,512]{2,1,0:T(8,128)S(1)} %shard_map.88), channel_id=1, replica_groups=mesh['walker'=32,'group'=4,'orb'=4] {'orb'}, dimensions={0} | all-to-all | bytes 1048576 | tf_op jit(solution)/shard_map/all_to_all | solution.py:430
  104.4 0.1 shard_map.89
  104.6 0.0 copy-start.2
  104.6 1.0 copy-done.2
  105.5 4.4 %all-to-all-start.2 = ((f32[16,32,512]{2,1,0:T(8,128)}), f32[16,32,512]{2,1,0:T(8,128)}, u32[]{:S(2)}, u32[]{:S(2)}) async-start(f32[16,32,512]{2,1,0:T(8,128)} %copy-done.2), calls=%async_computation.2 | async-start | bytes 2097152 | tf_op jit(solution)/shard_map/all_to_all | solution.py:430
  109.9 3.7 %collective-permute-start.5 = (f32[4,32,512]{2,1,0:T(8,128)S(1)}, f32[4,32,512]{2,1,0:T(8,128)S(1)}, u32[]{:S(2)}, u32[]{:S(2)}) collective-permute-start(f32[4,32,512]{2,1,0:T(8,128)S(1)} %get-tuple-element.11.own_ref), channel_id=1, source_target_pairs={{0,8},{4,12},{8,0},{12,4},{1,9},{5,13},{9,1},{13,5},{2,10},{6,14},... | collective-permute-start | bytes 786440 | tf_op jit(solution)/shard_map/ppermute | solution.py:434
  113.6 16.1 %collective-permute-done.5.far_ref = f32[4,32,512]{2,1,0:T(8,128)S(1)} collective-permute-done((f32[4,32,512]{2,1,0:T(8,128)S(1)}, f32[4,32,512]{2,1,0:T(8,128)S(1)}, u32[]{:S(2)}, u32[]{:S(2)}) %collective-permute-start.5) | collective-permute-done | bytes 262176 | tf_op jit(solution)/shard_map/ppermute | solution.py:434
  129.8 1.9 collective-permute-start.6
  131.7 1.9 collective-permute-done.6.pair_ref
  133.6 0.9 copy-done.4
  134.5 2.8 %shard_map.91.refs_1_.own_ref = f32[128,512]{1,0:T(8,128)S(1)} custom-call(s32[2]{0:T(128)S(1)} %pad_add_fusion.place_ref, f32[4,32,512]{2,1,0:T(8,128)S(1)} %copy-done.4, f32[4,32,512]{2,1,0:T(8,128)S(1)} %collective-permute-done.5.far_ref, f32[2,4,32,512]{3,2,1,0:T(8,128)S(1)} %collective-permute-done.6.pair_ref, f32[512,512]{1,0:T(8,128)S(1)} %copy-done.1, ...), custom_call_target="tpu_custom_call" | custom-call | flops 1073741824 | bytes 1048576 | tf_op jit(solution)/shard_map/pallas_call | solution.py:50
  137.4 4.7 %collective-permute-start.9 = (f32[128,512]{1,0:T(8,128)S(1)}, f32[128,512]{1,0:T(8,128)}, u32[]{:S(2)}, u32[]{:S(2)}) collective-permute-start(f32[128,512]{1,0:T(8,128)S(1)} %shard_map.91.refs_1_.own_ref), channel_id=1, source_target_pairs={{0,3},{1,2},{2,1},{3,0},{4,7},{5,6},{6,5},{7,4},{8,11},{9,10},{10,... | collective-permute-start | bytes 786440 | tf_op jit(solution)/shard_map/ppermute | solution.py:434
  142.1 2.7 %collective-permute-start.8 = (f32[128,512]{1,0:T(8,128)S(1)}, f32[128,512]{1,0:T(8,128)}, u32[]{:S(2)}, u32[]{:S(2)}) collective-permute-start(f32[128,512]{1,0:T(8,128)S(1)} %shard_map.91.refs_1_.own_ref), channel_id=1, source_target_pairs={{0,2},{1,3},{2,0},{3,1},{4,6},{5,7},{6,4},{7,5},{8,10},{9,11},{10,... | collective-permute-start | bytes 786440 | tf_op jit(solution)/shard_map/ppermute | solution.py:434
  144.8 2.5 %collective-permute-start.7 = (f32[128,512]{1,0:T(8,128)S(1)}, f32[128,512]{1,0:T(8,128)}, u32[]{:S(2)}, u32[]{:S(2)}) collective-permute-start(f32[128,512]{1,0:T(8,128)S(1)} %shard_map.91.refs_1_.own_ref), channel_id=1, source_target_pairs={{0,1},{1,0},{2,3},{3,2},{4,5},{5,4},{6,7},{7,6},{8,9},{9,8},{10,11... | collective-permute-start | bytes 786440 | tf_op jit(solution)/shard_map/ppermute | solution.py:434
  147.2 0.0 copy-start.15
  147.2 1.2 copy-done.15
  148.5 1.8 shard_map.90.refs_0_
  150.2 15.3 %all-to-all-start.3 = ((f32[128,1,128]{2,1,0:T(1,128)}), f32[128,1,128]{2,1,0:T(1,128)S(1)}, u32[]{:S(2)}, u32[]{:S(2)}) async-start(f32[128,1,128]{2,1,0:T(1,128)} %bitcast.13), calls=%async_computation.3 | async-start | bytes 131072 | tf_op jit(solution)/shard_map/all_to_all | solution.py:430
  165.5 1.2 copy-done.7
  166.7 14.4 %shard_map.92.left_ref = f32[512,512]{1,0:T(8,128)S(1)} custom-call(f32[512,512]{1,0:T(8,128)} %bitcast.9.refs_0_.core_ref, f32[512,512]{1,0:T(8,128)S(1)} %bitcast.21, f32[128,128]{1,0:T(8,128)} %shard_map.90.refs_0_, f32[128,512]{1,0:T(8,128)S(1)} %shard_map.91.refs_1_.own_ref), custom_call_target="tpu_custom_call" | custom-call | flops 17179869184 | bytes 1048576 | tf_op jit(solution)/shard_map/pallas_call | solution.py:50
  181.2 0.9 shard_map.94
  182.1 4.3 %all-to-all-start.4 = ((f32[4,16,128]{2,1,0:T(8,128)}), f32[4,16,128]{2,1,0:T(8,128)S(1)}, u32[]{:S(2)}, u32[]{:S(2)}) async-start(f32[4,16,128]{2,1,0:T(8,128)} %shard_map.94), calls=%async_computation.4 | async-start | bytes 65536 | tf_op jit(solution)/shard_map/all_to_all | solution.py:430
  186.5 3.1 %shard_map.93 = f32[512,512]{1,0:T(8,128)} custom-call(s32[2]{0:T(128)S(1)} %pad_add_fusion.place_ref, f32[512,512]{1,0:T(8,128)S(1)} %copy-done.1, f32[512,512]{1,0:T(8,128)S(1)} %shard_map.92.left_ref, f32[128,512]{1,0:T(8,128)S(1)} %shard_map.91.refs_1_.own_ref, f32[128,512]{1,0:T(8,128)} %collective-permute-done.7.refs_0_, ...), custom_call_target="tpu_custom_call" | custom-call | flops 1073741824 | bytes 1048576 | tf_op jit(solution)/shard_map/pallas_call | solution.py:50
  189.6 2.3 %all-to-all-done.4.parts_ref = f32[4,16,128]{2,1,0:T(8,128)S(1)} async-done(((f32[4,16,128]{2,1,0:T(8,128)}), f32[4,16,128]{2,1,0:T(8,128)S(1)}, u32[]{:S(2)}, u32[]{:S(2)}) %all-to-all-start.4) | async-done | bytes 32800 | tf_op jit(solution)/shard_map/all_to_all | solution.py:430
  191.9 0.6 shard_map.95
  (32 shorter events, 0.1 us)
Async XLA Ops:
  0.6 0.7 copy-start.16
  0.6 0.7 copy-start.13
  1.3 1.2 copy-start
  2.5 1.2 copy-start.14
  3.8 0.7 copy-start.17
  4.4 0.7 copy-start.18
  7.3 72.1 %copy-start.9 = (f32[128,512]{1,0:T(8,128)}, f32[128,512]{1,0:T(8,128)S(1)}, u32[]{:S(2)}) copy-start(f32[128,512]{1,0:T(8,128)S(1)} %get-tuple-element.8.own_ref) | copy-start | bytes 786436
  7.3 19.8 %copy-start.1 = (f32[512,512]{1,0:T(8,128)S(1)}, f32[512,512]{1,0:T(8,128)}, u32[]{:S(2)}) copy-start(f32[512,512]{1,0:T(8,128)} %inverse_ref.3) | copy-start | bytes 3145732
  7.3 81.1 %all-to-all-start = ((f32[128,16,128]{2,1,0:T(8,128)}), f32[128,16,128]{2,1,0:T(8,128)S(1)}, u32[]{:S(2)}, u32[]{:S(2)}) async-start(f32[128,16,128]{2,1,0:T(8,128)} %bitcast.4), calls=%async_computation | async-start | bytes 2097152 | tf_op jit(solution)/shard_map/all_to_all | solution.py:430
  27.1 61.4 %collective-permute-start.4 = (f32[512,512]{1,0:T(8,128)S(1)}, f32[512,512]{1,0:T(8,128)S(1)}, u32[]{:S(2)}, u32[]{:S(2)}) collective-permute-start(f32[512,512]{1,0:T(8,128)S(1)} %copy-done.1), channel_id=1, source_target_pairs={{0,3},{1,2},{2,1},{3,0},{4,7},{5,6},{6,5},{7,4},{8,11},{9,10},{10,... | collective-permute-start | bytes 3145736 | tf_op jit(solution)/shard_map/ppermute | solution.py:434
  31.7 56.7 %collective-permute-start.3 = (f32[512,512]{1,0:T(8,128)S(1)}, f32[512,512]{1,0:T(8,128)}, u32[]{:S(2)}, u32[]{:S(2)}) collective-permute-start(f32[512,512]{1,0:T(8,128)S(1)} %copy-done.1), channel_id=1, source_target_pairs={{0,2},{1,3},{2,0},{3,1},{4,6},{5,7},{6,4},{7,5},{8,10},{9,11},{10,... | collective-permute-start | bytes 3145736 | tf_op jit(solution)/shard_map/ppermute | solution.py:434
  34.5 54.0 %collective-permute-start.2 = (f32[512,512]{1,0:T(8,128)S(1)}, f32[512,512]{1,0:T(8,128)}, u32[]{:S(2)}, u32[]{:S(2)}) collective-permute-start(f32[512,512]{1,0:T(8,128)S(1)} %copy-done.1), channel_id=1, source_target_pairs={{0,1},{1,0},{2,3},{3,2},{4,5},{5,4},{6,7},{7,6},{8,9},{9,8},{10,11... | collective-permute-start | bytes 3145736 | tf_op jit(solution)/shard_map/ppermute | solution.py:434
  36.9 42.5 %collective-permute-start = (f32[128,512]{1,0:T(8,128)S(1)}, f32[128,512]{1,0:T(8,128)S(1)}, u32[]{:S(2)}, u32[]{:S(2)}) collective-permute-start(f32[128,512]{1,0:T(8,128)S(1)} %get-tuple-element.8.own_ref), channel_id=1, source_target_pairs={{0,8},{4,12},{8,0},{12,4},{1,9},{5,13},{9,1},{13,5},{2,10},{6,14},... | collective-permute-start | bytes 786440 | tf_op jit(solution)/shard_map/ppermute | solution.py:434
  79.4 0.9 copy-start.11
  80.3 4.1 %collective-permute-start.1 = (f32[2,128,512]{2,1,0:T(8,128)}, f32[2,128,512]{2,1,0:T(8,128)}, u32[]{:S(2)}, u32[]{:S(2)}) collective-permute-start(f32[2,128,512]{2,1,0:T(8,128)} %pad_maximum_fusion), channel_id=1, source_target_pairs={{0,4},{4,0},{8,12},{12,8},{1,5},{5,1},{9,13},{13,9},{2,6},{6,2},{1... | collective-permute-start | bytes 1572872 | tf_op jit(solution)/shard_map/ppermute | solution.py:434
  82.3 6.2 %copy-start.8 = (f32[128,512]{1,0:T(8,128)S(1)}, f32[128,512]{1,0:T(8,128)}, u32[]{:S(2)}) copy-start(f32[128,512]{1,0:T(8,128)} %old_ref.1) | copy-start | bytes 786436
  84.4 1.0 copy-start.10
  85.4 0.9 copy-start.12
  87.4 1.0 copy-start.5
  88.5 1.2 copy-start.6
  104.6 1.0 copy-start.2
  105.5 24.2 %copy-start.3 = (f32[4,32,512]{2,1,0:T(8,128)}, f32[4,32,512]{2,1,0:T(8,128)S(1)}, u32[]{:S(2)}) copy-start(f32[4,32,512]{2,1,0:T(8,128)S(1)} %get-tuple-element.11.own_ref) | copy-start | bytes 786436
  105.5 41.7 %all-to-all-start.2 = ((f32[16,32,512]{2,1,0:T(8,128)}), f32[16,32,512]{2,1,0:T(8,128)}, u32[]{:S(2)}, u32[]{:S(2)}) async-start(f32[16,32,512]{2,1,0:T(8,128)} %copy-done.2), calls=%async_computation.2 | async-start | bytes 2097152 | tf_op jit(solution)/shard_map/all_to_all | solution.py:430
  109.9 19.8 %collective-permute-start.5 = (f32[4,32,512]{2,1,0:T(8,128)S(1)}, f32[4,32,512]{2,1,0:T(8,128)S(1)}, u32[]{:S(2)}, u32[]{:S(2)}) collective-permute-start(f32[4,32,512]{2,1,0:T(8,128)S(1)} %get-tuple-element.11.own_ref), channel_id=1, source_target_pairs={{0,8},{4,12},{8,0},{12,4},{1,9},{5,13},{9,1},{13,5},{2,10},{6,14},... | collective-permute-start | bytes 786440 | tf_op jit(solution)/shard_map/ppermute | solution.py:434
  129.8 3.8 %collective-permute-start.6 = (f32[2,4,32,512]{3,2,1,0:T(8,128)S(1)}, f32[2,4,32,512]{3,2,1,0:T(8,128)S(1)}, u32[]{:S(2)}, u32[]{:S(2)}) collective-permute-start(f32[2,4,32,512]{3,2,1,0:T(8,128)S(1)} %pad_maximum_fusion.1), channel_id=1, source_target_pairs={{0,4},{4,0},{8,12},{12,8},{1,5},{5,1},{9,13},{13,9},{2,6},{6,2},{1... | collective-permute-start | bytes 1572872 | tf_op jit(solution)/shard_map/ppermute | solution.py:434
  133.6 1.0 copy-start.4
  137.4 49.1 %collective-permute-start.9 = (f32[128,512]{1,0:T(8,128)S(1)}, f32[128,512]{1,0:T(8,128)}, u32[]{:S(2)}, u32[]{:S(2)}) collective-permute-start(f32[128,512]{1,0:T(8,128)S(1)} %shard_map.91.refs_1_.own_ref), channel_id=1, source_target_pairs={{0,3},{1,2},{2,1},{3,0},{4,7},{5,6},{6,5},{7,4},{8,11},{9,10},{10,... | collective-permute-start | bytes 786440 | tf_op jit(solution)/shard_map/ppermute | solution.py:434
  142.1 44.3 %collective-permute-start.8 = (f32[128,512]{1,0:T(8,128)S(1)}, f32[128,512]{1,0:T(8,128)}, u32[]{:S(2)}, u32[]{:S(2)}) collective-permute-start(f32[128,512]{1,0:T(8,128)S(1)} %shard_map.91.refs_1_.own_ref), channel_id=1, source_target_pairs={{0,2},{1,3},{2,0},{3,1},{4,6},{5,7},{6,4},{7,5},{8,10},{9,11},{10,... | collective-permute-start | bytes 786440 | tf_op jit(solution)/shard_map/ppermute | solution.py:434
  144.8 41.7 %collective-permute-start.7 = (f32[128,512]{1,0:T(8,128)S(1)}, f32[128,512]{1,0:T(8,128)}, u32[]{:S(2)}, u32[]{:S(2)}) collective-permute-start(f32[128,512]{1,0:T(8,128)S(1)} %shard_map.91.refs_1_.own_ref), channel_id=1, source_target_pairs={{0,1},{1,0},{2,3},{3,2},{4,5},{5,4},{6,7},{7,6},{8,9},{9,8},{10,11... | collective-permute-start | bytes 786440 | tf_op jit(solution)/shard_map/ppermute | solution.py:434
  147.2 1.2 copy-start.15
  150.2 31.0 %all-to-all-start.3 = ((f32[128,1,128]{2,1,0:T(1,128)}), f32[128,1,128]{2,1,0:T(1,128)S(1)}, u32[]{:S(2)}, u32[]{:S(2)}) async-start(f32[128,1,128]{2,1,0:T(1,128)} %bitcast.13), calls=%async_computation.3 | async-start | bytes 131072 | tf_op jit(solution)/shard_map/all_to_all | solution.py:430
  165.5 1.2 copy-start.7
  182.1 9.8 %all-to-all-start.4 = ((f32[4,16,128]{2,1,0:T(8,128)}), f32[4,16,128]{2,1,0:T(8,128)S(1)}, u32[]{:S(2)}, u32[]{:S(2)}) async-start(f32[4,16,128]{2,1,0:T(8,128)} %shard_map.94), calls=%async_computation.4 | async-start | bytes 65536 | tf_op jit(solution)/shard_map/all_to_all | solution.py:430
